TPU v7x, 32 devices: a whole 2x2x4 slice. The times are simulated.
32 devices in a mesh: grp: 2 (over y), tm: 4 (over z), tmpl: 4 (over x, core).
Axes of the slice: x: 2, y: 2, z: 4, core: 2. Of those that a mesh axis runs over, the one named last changes fastest.
Arguments:
- records: bfloat16 [160, 3072], P(None, ('grp', 'tm')), parts along dimension 1, may hold values from -600 to 600
- templates: bfloat16 [160, 4, 4, 200], P(None, 'tm', 'tmpl'), may hold values from -60 to 60
- channel_mask: int32 [160, 4, 4], P(None, 'tm', 'tmpl'), may hold values 0 or 1
- lag_table: int32 [160, 4, 4], P(None, 'tm', 'tmpl'), may hold values from 0 to 63
Outputs:
- stacked: float32 [4, 4, 3072], P(None, 'tmpl', ('grp', 'tm')), parts along dimension 2
There are 2 independent parts, one for each index of `grp`. A program takes and returns all parts, laid end to end along the dimension named above; an argument that names none is the same for every part. Nothing has to cross between parts.
All inputs are finite; a program needn't handle non-finite values. No bound on the sum of `channel_mask` on one device may be relied on, other than what follows from the above.
Results may differ from a plain program's by a relative error of at most 0.0003.
Values may be sent and summed in bfloat16 or wider, within the bound.
A program may use at most 192 MiB of HBM per device.

v0:
```python
import functools

import jax
import jax.numpy as jnp
from jax import lax
from jax.experimental import pallas as pl
from jax.experimental.pallas import tpu as pltpu
from jax.sharding import PartitionSpec as P

LAGS = 64
LANES = 128
STEP = 32
ROWS = 16


def up(value, unit):
    return -(-value // unit) * unit


def shifted_left(values, count):
    width = values.shape[1]
    if count % width == 0:
        return values
    return pltpu.roll(values, width - count % width, 1)


def window_sum(values, length):
    total, done, power, span = None, 0, values, 1
    while True:
        if length & span:
            part = shifted_left(power, done)
            total = part if total is None else total + part
            done += span
        if span * 2 > length:
            return total
        power = power + shifted_left(power, span)
        span *= 2


def correlate(tmpl_len, count, ext_ref, tmpl_ref, code_ref, out_ref, wide_ref, trace_ref, spread_ref):
    channels, ext_len = ext_ref.shape
    slab_len = out_ref.shape[1]
    tmpl_pad = tmpl_ref.shape[2]
    span = trace_ref.shape[2]
    blocks = -(-tmpl_len // STEP)
    wide = blocks * STEP * ROWS
    deep = STEP * ROWS
    reach = up(slab_len + LAGS - 1 + (blocks - 1) * STEP, LANES)

    lane = lax.broadcasted_iota(jnp.int32, (tmpl_pad, wide), 1)
    sample = lax.broadcasted_iota(jnp.int32, (tmpl_pad, wide), 0)
    spread_ref[...] = jnp.where(lane // ROWS == sample, 1.0, 0.0).astype(jnp.bfloat16)
    own = lax.broadcasted_iota(jnp.int32, (channels, wide), 1) % ROWS == (
        lax.broadcasted_iota(jnp.int32, (channels, wide), 0) % ROWS
    )
    for n in range(count):
        widened = jnp.dot(tmpl_ref[n], spread_ref[...], preferred_element_type=jnp.float32)
        wide_ref[n] = jnp.where(own, widened, 0.0).astype(jnp.bfloat16)

    @pl.loop(0, channels // ROWS)
    def _(group):
        rows = pl.ds(pl.multiple_of(group * ROWS, ROWS), ROWS)
        series = ext_ref[rows, :]
        as_float = series.astype(jnp.float32)
        energy = window_sum(as_float * as_float, tmpl_len)[:, :span]
        inverse_rms = lax.rsqrt(energy / tmpl_len + 1e-05)
        moved = jnp.concatenate(
            [shifted_left(as_float, b)[:, :reach].astype(jnp.bfloat16) for b in range(STEP)], axis=0
        )
        for n in range(count):
            left = jnp.concatenate(
                [wide_ref[n, rows, a * deep : (a + 1) * deep] for a in range(blocks)], axis=0
            )
            partial = jnp.dot(left, moved, preferred_element_type=jnp.float32)
            per_tile = LANES // STEP
            total = None
            for phase in range(min(per_tile, blocks)):
                lined = None
                for a in range(phase, blocks, per_tile):
                    start = (a - phase) * STEP
                    piece = partial[a * ROWS : (a + 1) * ROWS, start:]
                    piece = piece[:, : min(span + LANES, reach - start)]
                    if piece.shape[1] < span + LANES:
                        piece = jnp.concatenate(
                            [piece, jnp.zeros((ROWS, span + LANES - piece.shape[1]), jnp.float32)],
                            axis=1,
                        )
                    lined = piece if lined is None else lined + piece
                lined = shifted_left(lined, phase * STEP)[:, :span]
                total = lined if total is None else total + lined
            kernel = tmpl_ref[n, rows, :].astype(jnp.float32)
            mean = jnp.sum(kernel * kernel, axis=1, keepdims=True) / tmpl_len
            weight = 1.0 / (jnp.sqrt(mean + 1e-05) * tmpl_len)
            trace_ref[n, rows, :] = total * inverse_rms * weight

    lag = LAGS - 1 - lax.broadcasted_iota(jnp.int32, (LAGS, channels), 0)
    for n in range(count):
        pick = jnp.where(code_ref[n, 0:1, :channels] == lag, 1.0, 0.0).astype(jnp.bfloat16)
        trace = trace_ref[n]
        high = trace.astype(jnp.bfloat16)
        low = (trace - high.astype(jnp.float32)).astype(jnp.bfloat16)
        by_lag = jnp.dot(pick, high, preferred_element_type=jnp.float32)
        by_lag += jnp.dot(pick, low, preferred_element_type=jnp.float32)
        lined = pltpu.roll(by_lag, span - LAGS + 1, 1, stride=1, stride_axis=0)
        out_ref[n : n + 1, :] = jnp.sum(lined, axis=0, keepdims=True)[:, :slab_len]


def local(records, templates, channel_mask, lag_table):
    channels, slab_len = records.shape
    tmpl_len = templates.shape[3]
    second = templates.shape[2]
    tmpl_pad = up(tmpl_len, LANES)
    size = lax.axis_size("tm")
    count = size * templates.shape[1] * second
    span = up(slab_len + LAGS - 1, LANES)
    blocks = -(-tmpl_len // STEP)
    wide = blocks * STEP * ROWS
    tail = lax.ppermute(records, "tm", [(i + 1, i) for i in range(size - 1)])
    extended = jnp.concatenate([records, tail], axis=1)
    rows = jnp.transpose(templates, (1, 2, 0, 3)).reshape(-1, channels, tmpl_len)
    rows = jnp.pad(rows, ((0, 0), (0, 0), (0, tmpl_pad - tmpl_len)))
    code = jnp.where(channel_mask != 0, lag_table, -1)
    code = jnp.transpose(code, (1, 2, 0)).reshape(-1, 1, channels)
    rows = lax.all_gather(rows, "tm", axis=0, tiled=True)
    code = lax.all_gather(code, "tm", axis=0, tiled=True)
    out = pl.pallas_call(
        functools.partial(correlate, tmpl_len, count),
        out_shape=jax.ShapeDtypeStruct((count, slab_len), jnp.float32),
        in_specs=[pl.BlockSpec(memory_space=pltpu.VMEM)] * 3,
        out_specs=pl.BlockSpec(memory_space=pltpu.VMEM),
        scratch_shapes=[
            pltpu.VMEM((count, channels, wide), jnp.bfloat16),
            pltpu.VMEM((count, channels, span), jnp.float32),
            pltpu.VMEM((tmpl_pad, wide), jnp.bfloat16),
        ],
        compiler_params=pltpu.CompilerParams(vmem_limit_bytes=56 << 20),
    )(extended, rows, code)
    return out.reshape(count // second, second, slab_len)


def solution(mesh):
    return jax.shard_map(
        local,
        mesh=mesh,
        in_specs=(
            P(None, ("grp", "tm")),
            P(None, "tm", "tmpl", None),
            P(None, "tm", "tmpl"),
            P(None, "tm", "tmpl"),
        ),
        out_specs=P(None, "tmpl", ("grp", "tm")),
        check_vma=False,
    )
```

profile of v0, /device:TPU:0, one launch (start us, length us, event | category | flops | bytes accessed | tf_op | source)
XLA Modules:
  0.0 46.5 jit_solution(18144395571377952099)
XLA Ops:
  0.0 1.3 %collective-permute-start = (bf16[160,384]{1,0:T(8,128)(2,1)}, bf16[160,384]{1,0:T(8,128)(2,1)S(1)}, u32[]{:S(2)}, u32[]{:S(2)}) collective-permute-start(bf16[160,384]{1,0:T(8,128)(2,1)} %param.4), channel_id=1, source_target_pairs={{4,0},{8,4},{12,8},{5,1},{9,5},{13,9},{6,2},{10,6},{14,10},{7,3},{... | collective-permute-start | bytes 368648 | tf_op jit(solution)/shard_map/ppermute | solution.py:118
  1.3 0.0 copy-start.2
  1.3 0.0 copy-start.1
  1.3 0.7 %copy-done.2 = s32[160,1,1]{0,2,1:T(1,128)S(1)} copy-done((s32[160,1,1]{0,2,1:T(1,128)S(1)}, s32[160,1,1]{0,2,1:T(1,128)}, u32[]{:S(2)}) %copy-start.2) | copy-done | bytes 664
  2.0 0.0 copy-done.1
  2.0 0.0 copy-start.3
  2.0 0.7 %copy-done.3 = u32[32]{0:T(128)S(1)} copy-done((u32[32]{0:T(128)S(1)}, u32[32]{0:T(128)}, u32[]{:S(2)}) %copy-start.3) | copy-done | bytes 152
  2.6 0.6 %dynamic-slice = u32[1]{0:T(128)} dynamic-slice(u32[32]{0:T(128)S(1)} %copy-done.3, u32[]{:T(128)S(6)} %add.2), dynamic_slice_sizes={1} | dynamic-slice | bytes 12
  3.9 0.2 dynamic-update-slice
  4.1 11.0 %all-reduce.1 = s32[640]{0:T(1024)S(1)} all-reduce(s32[640]{0:T(1024)S(1)} %dynamic-update-slice), channel_id=2, replica_groups=mesh['grp'=2,'tm'=4,'tmpl'=4] {'tm'}, use_global_device_ids=true, to_apply=%add.1 | all-reduce | flops 640 | bytes 5120
  15.1 0.7 %reshape.4.code_ref = s32[4,1,160]{2,1,0:T(1,128)} reshape(s32[640]{0:T(1024)S(1)} %all-reduce.1) | data formatting | bytes 5120 | tf_op jit(solution)/shard_map/all_gather | solution.py:125
  15.8 0.9 %pad.4 = bf16[1,160,256]{2,1,0:T(8,128)(2,1)S(1)} pad(bf16[1,160,200]{2,1,0:T(8,128)(2,1)} %bitcast.4, bf16[]{:T(256)} %constant.1.clone.1), padding=0_0x0_0x0_56 | pad | bytes 145922 | tf_op jit(solution)/shard_map/jit(_pad)/pad | solution.py:121
  16.7 0.0 copy-start
  16.7 15.1 %all_gather.6.tmpl_ref = bf16[4,160,256]{2,1,0:T(8,128)(2,1)} all-gather(bf16[1,160,256]{2,1,0:T(8,128)(2,1)S(1)} %pad.4), channel_id=1, replica_groups=mesh['grp'=2,'tm'=4,'tmpl'=4] {'tm'}, dimensions={0}, use_global_device_ids=true | all-gather | bytes 409600 | tf_op jit(solution)/shard_map/all_gather | solution.py:124
  31.8 0.0 collective-permute-done
  31.8 0.0 copy-done
  31.8 0.7 %pad_maximum_fusion.ext_ref = bf16[160,768]{1,0:T(8,128)(2,1)} fusion(bf16[160,384]{1,0:T(8,128)(2,1)S(1)} %collective-permute-done, bf16[160,384]{1,0:T(8,128)(2,1)S(1)} %copy-done), kind=kLoop, calls=%fused_computation | loop fusion | flops 491520 | bytes 491520 | tf_op jit(solution)/shard_map/concatenate | solution.py:119
  32.5 12.7 %shard_map.46 = f32[4,384]{1,0:T(4,128)} custom-call(bf16[160,768]{1,0:T(8,128)(2,1)} %pad_maximum_fusion.ext_ref, bf16[4,160,256]{2,1,0:T(8,128)(2,1)} %all_gather.6.tmpl_ref, s32[4,1,160]{2,1,0:T(1,128)} %reshape.4.code_ref), custom_call_target="tpu_custom_call" | custom-call | tf_op jit(solution)/shard_map/pallas_call | solution.py:126
  45.2 1.3 %copy.6 = f32[4,1,384]{2,1,0:T(1,128)} copy(f32[4,1,384]{2,0,1:T(4,128)} %bitcast.5) | data formatting | bytes 12288 | tf_op jit(solution)/shard_map/reshape | solution.py:138
  (2 shorter events, 0.0 us)
Async XLA Ops:
  0.0 31.8 %collective-permute-start = (bf16[160,384]{1,0:T(8,128)(2,1)}, bf16[160,384]{1,0:T(8,128)(2,1)S(1)}, u32[]{:S(2)}, u32[]{:S(2)}) collective-permute-start(bf16[160,384]{1,0:T(8,128)(2,1)} %param.4), channel_id=1, source_target_pairs={{4,0},{8,4},{12,8},{5,1},{9,5},{13,9},{6,2},{10,6},{14,10},{7,3},{... | collective-permute-start | bytes 368648 | tf_op jit(solution)/shard_map/ppermute | solution.py:118
  1.3 0.7 %copy-start.2 = (s32[160,1,1]{0,2,1:T(1,128)S(1)}, s32[160,1,1]{0,2,1:T(1,128)}, u32[]{:S(2)}) copy-start(s32[160,1,1]{0,2,1:T(1,128)} %param.6) | copy-start | bytes 1924
  1.3 0.7 %copy-start.1 = (s32[160,1,1]{0,2,1:T(1,128)S(1)}, s32[160,1,1]{0,2,1:T(1,128)}, u32[]{:S(2)}) copy-start(s32[160,1,1]{0,2,1:T(1,128)} %param.7) | copy-start | bytes 1924
  2.0 0.7 %copy-start.3 = (u32[32]{0:T(128)S(1)}, u32[32]{0:T(128)}, u32[]{:S(2)}) copy-start(u32[32]{0:T(128)} %constant.14) | copy-start | bytes 388
  16.7 15.1 %copy-start = (bf16[160,384]{1,0:T(8,128)(2,1)S(1)}, bf16[160,384]{1,0:T(8,128)(2,1)}, u32[]{:S(2)}) copy-start(bf16[160,384]{1,0:T(8,128)(2,1)} %param.4) | copy-start | bytes 368644
where the time goes:
time: 46.8 us; the launch traced here: 46.5 us
  blocking collectives  26.1 us (56%)
  Pallas kernels  12.7 us (27%)
  local copies, waits for them, and re-layouts  5.03 us (11%)
  starting transfers between devices  1.28 us (3%)
  other arithmetic  0.72 us (2%)
  between operations  0.71 us (2%)
    all_gather x1, blocking collectives, local(): rows = lax.all_gather(rows, 'tm', axis=0, tiled=True)  15.1 us
    pallas_call x1, Pallas kernels, local(): pl.pallas_call(functools.partial(correlate, tmpl_len, count), out_shape=j...  12.7 us
    unnamed x1, blocking collectives  11 us
    unnamed x11, local copies, waits for them, and re-layouts  2.17 us
    reshape x1, local copies, waits for them, and re-layouts, local(): return out.reshape(count // second, second, slab_len)  1.29 us
    ppermute x1, starting transfers between devices, local(): tail = lax.ppermute(records, 'tm', [(i + 1, i) for i in range(size - 1)])  1.28 us
  transfers between devices with their start and end apart: 1, of which 0 were waited for; matrix products, arithmetic and copies ran while one was open for 5% of the time, Pallas kernels for 0%

commit v1 on v0

v1 whole, which is shorter than its diff:
```python
import math

import jax
import jax.numpy as jnp
from jax import lax
from jax.experimental import pallas as pl
from jax.experimental.pallas import tpu as pltpu
from jax.sharding import PartitionSpec as P

LAGS = 64
LANES = 128
STEP = 32
ROWS = 16
GROUP = 8


def up(value, unit):
    return -(-value // unit) * unit


def shifted_left(values, count):
    width = values.shape[1]
    if count % width == 0:
        return values
    return pltpu.roll(values, width - count % width, 1)


def window_sum(values, length):
    total, done, power, span = None, 0, values, 1
    while True:
        if length & span:
            part = shifted_left(power, done)
            total = part if total is None else total + part
            done += span
        if span * 2 > length:
            return total
        power = power + shifted_left(power, span)
        span *= 2


def exchange(rec_ref, tmpl_ref, code_ref, tail_ref, slots_ref, codes_ref, sems):
    channels = rec_ref.shape[0]
    tm_size, grp_size = lax.axis_size("tm"), lax.axis_size("grp")
    me, part, col = lax.axis_index("tm"), lax.axis_index("grp"), lax.axis_index("tmpl")
    mate = col + 1 - 2 * (col % 2)
    share, half = channels // grp_size, channels // 2

    def there(axis, index):
        return {"device_id": {axis: index}, "device_id_type": pl.DeviceIdType.MESH}

    def copy(src, dst, name, index, where):
        send, recv = sems[name]
        return pltpu.make_async_remote_copy(
            src_ref=src, dst_ref=dst, send_sem=send.at[index], recv_sem=recv.at[index], **where
        )

    tm_peer = [(me + d) % tm_size for d in range(tm_size)]
    grp_peer = [(part + d) % grp_size for d in range(grp_size)]
    mine = pl.ds(pl.multiple_of(part * share, ROWS), share)
    piece = pl.ds(pl.multiple_of((col % 2) * half, ROWS), half)

    barrier = pltpu.get_barrier_semaphore()
    for d in range(1, tm_size):
        pl.semaphore_signal(barrier, inc=1, **there("tm", tm_peer[d]))
    for d in range(1, grp_size):
        pl.semaphore_signal(barrier, inc=1, **there("grp", grp_peer[d]))
    pl.semaphore_signal(barrier, inc=1, **there("tmpl", mate))

    rim = copy(rec_ref.at[piece], tail_ref.at[piece], "rim", 0, there("tm", jnp.maximum(me - 1, 0)))
    rim_on = copy(tail_ref.at[piece], tail_ref.at[piece], "rim", 1, there("tmpl", mate))
    sent = [
        copy(tmpl_ref.at[mine], slots_ref.at[d, mine], "tmpl", d, there("tm", tm_peer[d]))
        for d in range(1, tm_size)
    ]
    coded = [
        copy(code_ref, codes_ref.at[d], "code", d, there("tm", tm_peer[d])) for d in range(1, tm_size)
    ]
    passed = [
        [
            copy(
                slots_ref.at[d, mine],
                slots_ref.at[d, mine],
                "pass",
                d * grp_size + e,
                there("grp", grp_peer[e]),
            )
            for e in range(1, grp_size)
        ]
        for d in range(1, tm_size)
    ]

    def start():
        pl.semaphore_wait(barrier, tm_size + grp_size - 1)

        @pl.when(me > 0)
        def _():
            rim.start()

        for move in sent + coded:
            move.start()

    def land_rim():
        @pl.when(me < tm_size - 1)
        def _():
            rim.wait_recv()
            rim_on.start()
            rim_on.wait_recv()

        @pl.when(me == tm_size - 1)
        def _():
            tail_ref[...] = jnp.zeros_like(tail_ref)

    def pass_on():
        for move, onward in zip(sent, passed):
            move.wait_recv()
            for step in onward:
                step.start()

    def finish():
        for onward in passed:
            for step in onward:
                step.wait_recv()
        for move in coded:
            move.wait_recv()

    def drain():
        for move in sent + coded + [step for onward in passed for step in onward]:
            move.wait_send()

        @pl.when(me > 0)
        def _():
            rim.wait_send()

        @pl.when(me < tm_size - 1)
        def _():
            rim_on.wait_send()

    return start, land_rim, pass_on, finish, drain


def correlate(
    rec_ref,
    tmpl_ref,
    code_ref,
    out_ref,
    tail_ref,
    slots_ref,
    codes_ref,
    wide_ref,
    trace_ref,
    spread_ref,
    moved_ref,
    inverse_ref,
    *sem_refs,
):
    count, channels, tmpl_len = slots_ref.shape
    slab_len = rec_ref.shape[1]
    span = trace_ref.shape[2]
    blocks = -(-tmpl_len // STEP)
    wide = blocks * STEP * GROUP
    deep = STEP * GROUP
    reach = moved_ref.shape[2]
    per_tile = LANES // STEP
    batch = math.gcd(count, 4)
    names = ("rim", "tmpl", "code", "pass")
    sems = {name: sem_refs[2 * i : 2 * i + 2] for i, name in enumerate(names)}
    start, land_rim, pass_on, finish, drain = exchange(
        rec_ref, tmpl_ref, code_ref, tail_ref, slots_ref, codes_ref, sems
    )
    start()

    lane = lax.broadcasted_iota(jnp.int32, (tmpl_len, wide), 1)
    sample = lax.broadcasted_iota(jnp.int32, (tmpl_len, wide), 0)
    spread_ref[...] = jnp.where(lane // GROUP == sample, 1.0, 0.0).astype(jnp.bfloat16)
    slots_ref[0] = tmpl_ref[...]
    codes_ref[0] = code_ref[...]
    own = lax.broadcasted_iota(jnp.int32, (channels, wide), 1) % GROUP == (
        lax.broadcasted_iota(jnp.int32, (channels, wide), 0) % GROUP
    )

    def expand(n):
        kernel = slots_ref[n]
        widened = jnp.dot(kernel, spread_ref[...], preferred_element_type=jnp.float32)
        as_float = kernel.astype(jnp.float32)
        mean = jnp.sum(as_float * as_float, axis=1, keepdims=True) / tmpl_len
        weight = 1.0 / (jnp.sqrt(mean + 1e-05) * tmpl_len)
        wide_ref[n] = jnp.where(own, widened, 0.0)
        trace_ref[n] = jnp.broadcast_to(weight, (channels, span))

    expand(0)
    land_rim()

    @pl.loop(0, channels // ROWS)
    def _(pair):
        rows = pl.ds(pl.multiple_of(pair * ROWS, ROWS), ROWS)
        series = jnp.concatenate([rec_ref[rows, :], tail_ref[rows, :]], axis=1).astype(jnp.float32)
        energy = window_sum(series * series, tmpl_len)[:, :span]
        inverse_ref[rows, :] = lax.rsqrt(energy / tmpl_len + 1e-05)
        for side in range(ROWS // GROUP):
            part = series[side * GROUP : (side + 1) * GROUP]
            moved_ref[pair * (ROWS // GROUP) + side] = jnp.concatenate(
                [shifted_left(part, b)[:, :reach] for b in range(STEP)], axis=0
            ).astype(jnp.bfloat16)

    pass_on()
    finish()
    for n in range(1, count):
        expand(n)

    @pl.loop(0, count // batch)
    def _(turn):
        @pl.loop(0, channels // GROUP)
        def _(group):
            rows = pl.ds(pl.multiple_of(group * GROUP, GROUP), GROUP)
            left = jnp.concatenate(
                [
                    wide_ref[turn * batch + n, rows, a * deep : (a + 1) * deep]
                    for n in range(batch)
                    for a in range(blocks)
                ],
                axis=0,
            ).astype(jnp.bfloat16)
            partial = jnp.dot(left, moved_ref[group], preferred_element_type=jnp.float32)
            inverse_rms = inverse_ref[rows, :]
            for n in range(batch):
                total = None
                for phase in range(min(per_tile, blocks)):
                    lined = None
                    for a in range(phase, blocks, per_tile):
                        begin = (a - phase) * STEP
                        line = (n * blocks + a) * GROUP
                        piece = partial[line : line + GROUP, begin : begin + span + LANES]
                        if piece.shape[1] < span + LANES:
                            missing = span + LANES - piece.shape[1]
                            piece = jnp.concatenate(
                                [piece, jnp.zeros((GROUP, missing), jnp.float32)], axis=1
                            )
                        lined = piece if lined is None else lined + piece
                    lined = shifted_left(lined, phase * STEP)[:, :span]
                    total = lined if total is None else total + lined
                slot = turn * batch + n
                trace_ref[slot, rows, :] = total * inverse_rms * trace_ref[slot, rows, :]

    me = lax.axis_index("tm")
    lag = LAGS - 1 - lax.broadcasted_iota(jnp.int32, (LAGS, channels), 0)
    for n in range(count):
        pick = jnp.where(codes_ref[n] == lag, 1.0, 0.0).astype(jnp.bfloat16)
        trace = trace_ref[n]
        high = trace.astype(jnp.bfloat16)
        low = (trace - high.astype(jnp.float32)).astype(jnp.bfloat16)
        by_lag = jnp.dot(pick, high, preferred_element_type=jnp.float32)
        by_lag += jnp.dot(pick, low, preferred_element_type=jnp.float32)
        lined = pltpu.roll(by_lag, span - LAGS + 1, 1, stride=1, stride_axis=0)
        row = (me + count - n) % count
        out_ref[pl.ds(row, 1), :] = jnp.sum(lined, axis=0, keepdims=True)[:, :slab_len]
    drain()


def local(records, templates, channel_mask, lag_table):
    channels, slab_len = records.shape
    first, second, tmpl_len = templates.shape[1:]
    assert first == 1 and second == 1
    size, grp_size = lax.axis_size("tm"), lax.axis_size("grp")
    span = up(slab_len + LAGS - 1, LANES)
    blocks = -(-tmpl_len // STEP)
    wide = blocks * STEP * GROUP
    reach = up(slab_len + LAGS - 1 + (blocks - 1) * STEP, LANES)
    code = jnp.where(channel_mask != 0, lag_table, -1).reshape(1, channels)
    dma = pltpu.SemaphoreType.DMA
    out = pl.pallas_call(
        correlate,
        out_shape=jax.ShapeDtypeStruct((size, slab_len), jnp.float32),
        in_specs=[pl.BlockSpec(memory_space=pltpu.VMEM)] * 3,
        out_specs=pl.BlockSpec(memory_space=pltpu.VMEM),
        scratch_shapes=[
            pltpu.VMEM((channels, slab_len), jnp.bfloat16),
            pltpu.VMEM((size, channels, tmpl_len), jnp.bfloat16),
            pltpu.VMEM((size, 1, channels), jnp.int32),
            pltpu.VMEM((size, channels, wide), jnp.float32),
            pltpu.VMEM((size, channels, span), jnp.float32),
            pltpu.VMEM((tmpl_len, wide), jnp.bfloat16),
            pltpu.VMEM((channels // GROUP, STEP * GROUP, reach), jnp.bfloat16),
            pltpu.VMEM((channels, span), jnp.float32),
            dma((2,)),
            dma((2,)),
            dma((size,)),
            dma((size,)),
            dma((size,)),
            dma((size,)),
            dma((size * grp_size,)),
            dma((size * grp_size,)),
        ],
        compiler_params=pltpu.CompilerParams(
            vmem_limit_bytes=60 << 20, collective_id=0, has_side_effects=True
        ),
    )(records, templates.reshape(channels, tmpl_len), code)
    return out.reshape(size, 1, slab_len)


def solution(mesh):
    return jax.shard_map(
        local,
        mesh=mesh,
        in_specs=(
            P(None, ("grp", "tm")),
            P(None, "tm", "tmpl", None),
            P(None, "tm", "tmpl"),
            P(None, "tm", "tmpl"),
        ),
        out_specs=P(None, "tmpl", ("grp", "tm")),
        check_vma=False,
    )
```

time: 46.8 us -> 33.1 us (0.71)
  blocking collectives: 26.1 us -> 0 us
  Pallas kernels: 12.7 us -> 29.6 us
  local copies, waits for them, and re-layouts: 5.03 us -> 1.97 us
  starting transfers between devices: 1.28 us -> 0 us
  between operations: 0.71 us -> 0.01 us
  other arithmetic: 0.72 us -> 1.24 us
    pallas_call x1, Pallas kernels: 12.7 us -> 29.6 us  [local(): pl.pallas_call(correlate, out_shape=jax.ShapeDtypeStruct((size, slab_len)...]
    all_gather x1 -> x0, blocking collectives: 15.1 us -> none  [local(): rows = lax.all_gather(rows, 'tm', axis=0, tiled=True)]
    unnamed x1 -> x0, blocking collectives: 11 us -> none
    unnamed x11 -> x2, local copies, waits for them, and re-layouts: 2.17 us -> 0.68 us
    ppermute x1 -> x0, starting transfers between devices: 1.28 us -> none  [local(): tail = lax.ppermute(records, 'tm', [(i + 1, i) for i in range(size - 1)])]
    reshape x0 -> x1, other arithmetic: none -> 1.24 us  [local(): code = jnp.where(channel_mask != 0, lag_table, -1).reshape(1, channels)]
    pad x1 -> x0, local copies, waits for them, and re-layouts: 0.9 us -> none  [local(): rows = jnp.pad(rows, ((0, 0), (0, 0), (0, tmpl_pad - tmpl_len)))]
    concatenate x1 -> x0, other arithmetic: 0.71 us -> none  [local(): extended = jnp.concatenate([records, tail], axis=1)]
  transfers between devices with their start and end apart: 1 -> 0, of which waited for: 0 -> 0; matrix products, arithmetic and copies ran while one was open for 5% -> 0% of each run, Pallas kernels for 0% -> 0%
where the time goes in v1:
time: 33.1 us; the launch traced here: 32.9 us
  Pallas kernels  29.6 us (89%)
  local copies, waits for them, and re-layouts  1.97 us (6%)
  other arithmetic  1.24 us (4%)
    pallas_call x1, Pallas kernels, local(): pl.pallas_call(correlate, out_shape=jax.ShapeDtypeStruct((size, slab_len)...  29.6 us
    reshape x1, local copies, waits for them, and re-layouts, local(): return out.reshape(size, 1, slab_len)  1.29 us
    reshape x1, other arithmetic, local(): code = jnp.where(channel_mask != 0, lag_table, -1).reshape(1, channels)  1.24 us
    unnamed x2, local copies, waits for them, and re-layouts  0.68 us

profile of v1, /device:TPU:0, one launch (start us, length us, event | category | flops | bytes accessed | tf_op | source)
XLA Modules:
  0.0 32.9 jit_solution(10360207357181806205)
XLA Ops:
  0.0 0.0 copy-start
  0.0 0.7 %copy-done = s32[160,1,1]{0,2,1:T(1,128)S(1)} copy-done((s32[160,1,1]{0,2,1:T(1,128)S(1)}, s32[160,1,1]{0,2,1:T(1,128)}, u32[]{:S(2)}) %copy-start) | copy-done | bytes 664
  0.7 1.2 %fusion.code_ref = s32[1,160]{1,0:T(1,128)} fusion(s32[160,1,1]{0,2,1:T(1,128)S(1)} %copy-done, s32[160,1,1]{0,2,1:T(1,128)} %param.6), kind=kLoop, calls=%fused_computation.1 | loop fusion | flops 320 | bytes 1920 | tf_op jit(solution)/shard_map/reshape | solution.py:268
  1.9 29.6 %shard_map.46 = f32[4,384]{1,0:T(4,128)} custom-call(bf16[160,384]{1,0:T(8,128)(2,1)} %rec_ref.1, bf16[160,200]{1,0:T(8,128)(2,1)} %bitcast.4, s32[1,160]{1,0:T(1,128)} %fusion.code_ref), custom_call_target="tpu_custom_call" | custom-call | tf_op jit(solution)/shard_map/pallas_call | solution.py:270
  31.6 1.3 %copy.5 = f32[4,1,384]{2,1,0:T(1,128)} copy(f32[4,1,384]{2,0,1:T(4,128)} %bitcast.5) | data formatting | bytes 12288 | tf_op jit(solution)/shard_map/reshape | solution.py:297
Async XLA Ops:
  0.0 0.7 %copy-start = (s32[160,1,1]{0,2,1:T(1,128)S(1)}, s32[160,1,1]{0,2,1:T(1,128)}, u32[]{:S(2)}) copy-start(s32[160,1,1]{0,2,1:T(1,128)} %param.7) | copy-start | bytes 1924
